TPU v7x, 128 devices: a whole 4x4x4 slice. The times are simulated.
128 devices in a mesh: seg: 8 (over y_lo, z), grp: 16 (over x, y_hi, core).
Axes of the slice: x: 4, y: 4 (y_hi: 2, y_lo: 2; y = y_hi * 2 + y_lo), z: 4, core: 2. Of those that a mesh axis runs over, the one named last changes fastest.
Arguments:
- frames_in: bfloat16 [128, 32, 120, 128], P(('seg', 'grp')), may hold values from -6 to 6
- spatial_weight: bfloat16 [9, 128, 128], replicated, may hold values from -0.1875 to 0.1875
- temporal_weight: bfloat16 [2, 5, 128, 128], replicated, may hold values from -0.25 to 0.25
- uniting_weight: bfloat16 [2, 128, 128], replicated, may hold values from -0.375 to 0.375
- key_index: int32 [8], replicated, may hold values from 0 to 15
- dilation: int32 [2], replicated, may hold values from 1 to 8, as said below
- cotangent: bfloat16 [128, 32, 120, 128], P(('seg', 'grp')), may hold values from -6 to 6
Outputs:
- united: bfloat16 [128, 32, 120, 128], P(('seg', 'grp'))
- grad_frames: bfloat16 [128, 32, 120, 128], P(('seg', 'grp'))
- grad_spatial: float32 [9, 128, 128], replicated
- grad_temporal: float32 [2, 5, 128, 128], replicated
- grad_uniting: float32 [2, 128, 128], replicated
Inputs may be any that keep to these rules, and one draw needn't show every extreme that they name: `key_index`: position of a segment's keyframe within its 16 frames. Exactly one layer uses dilation 8; the others use less.
All inputs are finite; a program needn't handle non-finite values.
Results may differ from a plain program's by a relative error of at most 0.0095.
Values may be sent and summed in bfloat16 or wider, within the bound.
A program may use at most 128 MiB of HBM per device.

v0:
```python
import jax
import jax.numpy as jnp
from jax import lax
from jax.sharding import PartitionSpec as P

LAYERS = 2
DMAX = 8


def from_root(value, axis, root):
    mine = lax.axis_index(axis) == root
    return lax.psum(jnp.where(mine, value, jnp.zeros_like(value)), axis)


def silu_grad(value):
    sigma = jax.nn.sigmoid(value)
    return sigma * (1.0 + value * (1.0 - sigma))


def inner(left, right):
    return lax.dot_general(
        left, right, (((0,), (0,)), ((), ())), preferred_element_type=jnp.float32
    )


def spatial_forward(frames, kernel):
    count, rows, cols, chans = frames.shape
    padded = jnp.pad(frames, ((0, 0), (1, 1), (1, 1), (0, 0)))
    total = jnp.zeros((count * rows * cols, chans), jnp.float32)
    for row_tap in range(3):
        for col_tap in range(3):
            piece = padded[:, row_tap : row_tap + rows, col_tap : col_tap + cols, :].reshape(
                -1, chans
            )
            total = total + jnp.dot(
                piece, kernel[3 * row_tap + col_tap], preferred_element_type=jnp.float32
            )
    return total.reshape(frames.shape)


def spatial_back(grads, kernel):
    count, rows, cols, chans = grads.shape
    padded = jnp.pad(grads, ((0, 0), (1, 1), (1, 1), (0, 0)))
    total = jnp.zeros((count * rows * cols, chans), jnp.float32)
    for row_tap in range(3):
        for col_tap in range(3):
            piece = padded[
                :, 2 - row_tap : 2 - row_tap + rows, 2 - col_tap : 2 - col_tap + cols, :
            ].reshape(-1, chans)
            total = total + jnp.dot(
                piece, kernel[3 * row_tap + col_tap].T, preferred_element_type=jnp.float32
            )
    return total.reshape(grads.shape)


def spatial_wgrad(frames, grads):
    count, rows, cols, chans = frames.shape
    padded = jnp.pad(frames, ((0, 0), (1, 1), (1, 1), (0, 0)))
    flat_grads = grads.reshape(-1, chans)
    result = []
    for row_tap in range(3):
        for col_tap in range(3):
            piece = padded[:, row_tap : row_tap + rows, col_tap : col_tap + cols, :].reshape(
                -1, chans
            )
            result.append(inner(piece, flat_grads))
    return jnp.stack(result)


def shifted(values, offset):
    padded = jnp.pad(values, ((2 * DMAX, 2 * DMAX), (0, 0), (0, 0)))
    start = 2 * DMAX + offset
    return lax.dynamic_slice_in_dim(padded, start, values.shape[0], 0)


def temporal_forward(acts, kernel, step_size):
    chans = acts.shape[2]
    total = jnp.zeros((acts.shape[0] * acts.shape[1], chans), jnp.float32)
    for tap in range(5):
        piece = shifted(acts, (tap - 2) * step_size).reshape(-1, chans)
        total = total + jnp.dot(piece, kernel[tap], preferred_element_type=jnp.float32)
    return total.reshape(acts.shape)


def temporal_back(grads, kernel, step_size):
    chans = grads.shape[2]
    total = jnp.zeros((grads.shape[0] * grads.shape[1], chans), jnp.float32)
    for tap in range(5):
        piece = shifted(grads, (2 - tap) * step_size).reshape(-1, chans)
        total = total + jnp.dot(piece, kernel[tap].T, preferred_element_type=jnp.float32)
    return total.reshape(grads.shape)


def temporal_wgrad(acts, grads, step_size):
    chans = acts.shape[2]
    flat_grads = grads.reshape(-1, chans)
    return jnp.stack(
        [
            inner(shifted(acts, (tap - 2) * step_size).reshape(-1, chans), flat_grads)
            for tap in range(5)
        ]
    )


def to_pixels(flat):
    return lax.all_to_all(flat, ("seg", "grp"), split_axis=1, concat_axis=0, tiled=True)


def to_frames(blocks):
    return lax.all_to_all(blocks, ("seg", "grp"), split_axis=0, concat_axis=1, tiled=True)


def all_sum(parts):
    flat = jnp.concatenate([p.reshape(-1) for p in parts])
    count = lax.axis_size(("seg", "grp"))
    chunk = flat.shape[0] // count
    pieces = lax.all_to_all(
        flat.reshape(count, chunk), ("seg", "grp"), split_axis=0, concat_axis=0, tiled=True
    )
    mine = jnp.sum(pieces, axis=0)
    spread = jnp.broadcast_to(mine[None], (count, chunk))
    whole = lax.all_to_all(spread, ("seg", "grp"), split_axis=0, concat_axis=0, tiled=True)
    whole = whole.reshape(-1)
    out = []
    offset = 0
    for p in parts:
        out.append(whole[offset : offset + p.size].reshape(p.shape))
        offset += p.size
    return out


def local(
    frames_in, spatial_weight, temporal_weight, uniting_weight, key_index, dilation, cotangent
):
    local_frames, rows, cols, chans = frames_in.shape
    pixels = rows * cols
    seg_count = lax.axis_size("seg")
    pre_spatial = spatial_forward(frames_in, spatial_weight)
    act_zero = jax.nn.silu(pre_spatial).astype(jnp.bfloat16).reshape(local_frames, pixels, chans)
    cot_local = cotangent.reshape(local_frames, pixels, chans)
    act_blocks = to_pixels(act_zero)
    cot_blocks = to_pixels(cot_local)
    acts = [act_blocks]
    total_frames = acts[0].shape[0]
    block = acts[0].shape[1]
    seg_frames = total_frames // seg_count
    pres = []
    for layer in range(LAYERS):
        pre = temporal_forward(acts[-1], temporal_weight[layer], dilation[layer])
        pres.append(pre)
        acts.append(jax.nn.silu(pre).astype(jnp.bfloat16))
    feat = acts[-1]
    feat_seg = feat.reshape(seg_count, seg_frames, block, chans)
    positions = jnp.arange(seg_frames, dtype=jnp.int32)
    onehot = positions[None, :] == key_index[:, None]
    keys = jnp.einsum(
        "ns,nspc->npc", onehot.astype(jnp.bfloat16), feat_seg, preferred_element_type=jnp.float32
    ).astype(jnp.bfloat16)
    key_full = jnp.broadcast_to(keys[:, None], feat_seg.shape).reshape(-1, chans)
    feat_flat = feat.reshape(-1, chans)
    key_part = jnp.dot(
        keys.reshape(-1, chans), uniting_weight[1], preferred_element_type=jnp.float32
    ).reshape(seg_count, 1, block, chans)
    main_part = jnp.dot(feat_flat, uniting_weight[0], preferred_element_type=jnp.float32)
    united_blocks = (
        (main_part.reshape(seg_count, seg_frames, block, chans) + key_part)
        .astype(jnp.bfloat16)
        .reshape(total_frames, block, chans)
    )
    united = to_frames(united_blocks)
    cot_flat = cot_blocks.reshape(-1, chans)
    grad_feat = jnp.dot(cot_flat, uniting_weight[0].T, preferred_element_type=jnp.float32)
    seg_cot = jnp.sum(
        cot_blocks.reshape(seg_count, seg_frames, block, chans).astype(jnp.float32), axis=1
    )
    key_term = jnp.dot(
        seg_cot.reshape(-1, chans),
        uniting_weight[1].T.astype(jnp.float32),
        precision=lax.Precision.HIGHEST,
    ).reshape(seg_count, 1, block, chans)
    placed = onehot.astype(jnp.float32)[:, :, None, None] * key_term
    grad_feat = grad_feat.reshape(seg_count, seg_frames, block, chans) + placed
    grad_feat = grad_feat.reshape(total_frames, block, chans)
    grad_uniting = jnp.stack([inner(feat_flat, cot_flat), inner(key_full, cot_flat)])
    grad_pre = (grad_feat * silu_grad(pres[-1])).astype(jnp.bfloat16)
    tgrads = [None] * LAYERS
    grad_act0 = None
    for layer in range(LAYERS - 1, -1, -1):
        tgrads[layer] = temporal_wgrad(acts[layer], grad_pre, dilation[layer])
        grad_act = temporal_back(grad_pre, temporal_weight[layer], dilation[layer])
        if layer > 0:
            grad_pre = (grad_act * silu_grad(pres[layer - 1])).astype(jnp.bfloat16)
        else:
            grad_act0 = grad_act.astype(jnp.bfloat16)
    grad_time = to_frames(grad_act0).reshape(frames_in.shape)
    grad_spre = (grad_time.astype(jnp.float32) * silu_grad(pre_spatial)).astype(jnp.bfloat16)
    grad_frames = spatial_back(grad_spre, spatial_weight).astype(jnp.bfloat16)
    grad_spatial = spatial_wgrad(frames_in, grad_spre)
    summed = all_sum((grad_spatial, jnp.stack(tgrads), grad_uniting))
    scale = 1.0 / jnp.sqrt(jnp.float32(total_frames * pixels))
    return (
        united.reshape(frames_in.shape),
        grad_frames,
        summed[0] * scale,
        summed[1] * scale,
        summed[2] * scale,
    )


def solution(mesh):
    placed = (
        P(("seg", "grp"), None, None, None),
        P(),
        P(),
        P(),
        P(),
        P(),
        P(("seg", "grp"), None, None, None),
    )
    return jax.shard_map(
        local,
        mesh=mesh,
        in_specs=placed,
        out_specs=(
            P(("seg", "grp"), None, None, None),
            P(("seg", "grp"), None, None, None),
            P(),
            P(),
            P(),
        ),
        check_vma=False,
    )
```

profile of v0, /device:TPU:1, one launch (start us, length us, event | category | flops | bytes accessed | tf_op | source)
XLA Modules:
  0.0 491.9 jit_solution(17420087802253160140)
XLA Ops:
  0.6 7.3 %pad_slice_fusion.8 = (bf16[1,32,120,128]{3,2,1,0:T(8,128)(2,1)S(1)}, bf16[1,32,120,128]{3,2,1,0:T(8,128)(2,1)S(1)}, bf16[1,32,120,128]{3,2,1,0:T(8,128)(2,1)S(1...) fusion(bf16[1,32,120,128]{3,2,1,0:T(8,128)(2,1)} %param.7), kind=kLoop, calls=%fused_computation.142 | loop fusion | bytes 8847360 | tf_op jit(solution)/shard_map/slice | solution.py:32
  12.9 16.0 %copy.296 = bf16[1,3840,128]{2,0,1:T(2,128)(2,1)} copy(bf16[1,3840,128]{2,1,0:T(8,128)(2,1)S(1)} %fusion.40) | data formatting | bytes 1966080 | tf_op jit(solution)/shard_map/convert_element_type | solution.py:139
  29.5 23.1 %reduce.5 = bf16[3840,128]{1,0:T(8,128)(2,1)} reduce(bf16[3840,1,128]{2,1,0:T(2,128)(2,1)} %bitcast.395, bf16[]{:T(256)} %broadcast.150), dimensions={1}, to_apply=%bitcast.387.reduce_sub_computation | reduce | bytes 1966082
  52.6 3.0 reshape.597
  55.6 12.3 %all-to-all-start = ((bf16[128,2,1920]{2,1,0:T(2,128)(2,1)}), bf16[128,2,1920]{2,1,0:T(2,128)(2,1)}, u32[]{:S(2)}, u32[]{:S(2)}) async-start(bf16[128,2,1920]{2,1,0:T(2,128)(2,1)} %reshape.597), calls=%async_computation | async-start | bytes 1966080 | tf_op jit(solution)/shard_map/all_to_all | solution.py:106
  76.5 9.9 %copy.295 = bf16[1,3840,128]{2,0,1:T(2,128)(2,1)} copy(bf16[1,3840,128]{2,1,0:T(8,128)(2,1)} %bitcast.418) | data formatting | bytes 1966080 | tf_op jit(solution)/shard_map/reshape | solution.py:140
  86.4 23.1 %reduce.6 = bf16[3840,128]{1,0:T(8,128)(2,1)} reduce(bf16[3840,1,128]{2,1,0:T(2,128)(2,1)} %bitcast.396, bf16[]{:T(256)} %broadcast.150), dimensions={1}, to_apply=%bitcast.386.reduce_sub_computation | reduce | bytes 1966082
  109.5 3.0 reshape.599
  114.4 10.7 %all-to-all-start.2 = ((bf16[128,2,1920]{2,1,0:T(2,128)(2,1)}), bf16[128,2,1920]{2,1,0:T(2,128)(2,1)}, u32[]{:S(2)}, u32[]{:S(2)}) async-start(bf16[128,2,1920]{2,1,0:T(2,128)(2,1)} %reshape.599), calls=%async_computation.2 | async-start | bytes 1966080 | tf_op jit(solution)/shard_map/all_to_all | solution.py:106
  125.2 4.1 reshape.598
  129.4 17.4 %bitcast_reduce_fusion.1 = bf16[3840,128]{1,0:T(8,128)(2,1)} fusion(bf16[3840,1,128]{2,1,0:T(2,128)(2,1)S(1)} %reshape.598), kind=kLoop, calls=%fused_computation.260 | loop fusion | bytes 1966080 | tf_op jit(solution)/shard_map/all_to_all | solution.py:106
  151.5 5.9 %pad_dynamic-slice_fusion.12 = (bf16[128,30,128]{0,2,1:T(8,128)(2,1)}, bf16[128,30,128]{0,2,1:T(8,128)(2,1)}, bf16[128,30,128]{0,2,1:T(8,128)(2,1)}, bf16[128,30,128]{0,2,1:T(8,128)(2,1)}) fusion(s32[]{:T(128)S(6)} %select_n.19, bf16[128,30,128]{0,2,1:T(8,128)(2,1)} %copy.205, s32[]{:T(128)S(6)} %select_n.17, s32[]{:T(128)S(6)} %select_n.18, s32[]{:T(128)S(6)} %select_n.16), kind=kLoop, calls=%fused_computation.46 | loop fusion | bytes 4915216 | tf_op jit(solution)/shard_map/dynamic_slice | solution.py:73
  157.4 2.6 copy.209
  162.2 2.6 copy.207
  167.1 2.6 copy.208
  171.9 2.6 copy.206
  182.3 2.7 multiply_convert_fusion.10
  186.2 2.7 reshape.525
  191.8 3.5 pad_dynamic-slice_fusion.8
  195.3 2.7 copy.215
  222.8 5.7 %reshape.600 = bf16[3840,1,128]{2,1,0:T(2,128)(2,1)} reshape(bf16[128,2,1920]{2,1,0:T(2,128)(2,1)} %all-to-all-done.2) | data formatting | bytes 1966080
  228.5 18.6 %bitcast_reduce_fusion = bf16[3840,128]{1,0:T(8,128)(2,1)} fusion(bf16[3840,1,128]{2,1,0:T(2,128)(2,1)} %reshape.600), kind=kLoop, calls=%fused_computation.259 | loop fusion | bytes 1966080 | tf_op jit(solution)/shard_map/all_to_all | solution.py:106
  250.9 5.0 %multiply_convert_fusion = (bf16[8,16,30,128]{3,2,1,0:T(8,128)(2,1)}, bf16[8,16,30,128]{3,2,1,0:T(8,128)(2,1)}, f32[8,16,30,128]{3,2,1,0:T(8,128)}) fusion(f32[8,16,30,128]{3,2,1,0:T(8,128)} %reshape.530, f32[8,30,128]{2,1,0:T(8,128)S(1)} %fusion.47, f32[8,16]{1,0:T(8,128)S(1)} %get-tuple-element.39, bf16[8,16,30,128]{3,2,1,0:T(8,128)(2,1)} %dot_general.221, ...), kind=kOutput, calls=%fused_computation.50 | convolution fusion | flops 132218880 | bytes 7049216 | tf_op jit(solution)/shard_map/dot_general | solution.py:172
  258.5 2.9 copy.219
  263.3 3.0 multiply_convert_fusion.8
  267.3 3.2 pad_dynamic-slice_fusion.4
  270.5 2.7 copy.223
  275.4 2.7 copy.221
  284.1 2.7 copy.220
  296.2 3.2 multiply_convert_fusion.5
  299.4 2.7 reshape.541
  302.1 2.9 copy.225
  305.0 3.0 multiply_convert_fusion.6
  309.1 3.5 pad_dynamic-slice_fusion
  314.8 3.0 convolution_bitcast_fusion.1
  321.6 3.1 convolution_bitcast_fusion
  355.3 10.2 %all-to-all-start.3 = ((bf16[128,30,128]{2,1,0:T(8,128)(2,1)}), bf16[128,30,128]{2,1,0:T(8,128)(2,1)}, u32[]{:S(2)}, u32[]{:S(2)}) async-start(bf16[128,30,128]{2,1,0:T(8,128)(2,1)} %convert_element_type.195), calls=%async_computation.3 | async-start | bytes 2097152 | tf_op jit(solution)/shard_map/all_to_all | solution.py:110
  371.1 13.0 %all-to-all-done.3 = bf16[128,30,128]{2,1,0:T(8,128)(2,1)} async-done(((bf16[128,30,128]{2,1,0:T(8,128)(2,1)}), bf16[128,30,128]{2,1,0:T(8,128)(2,1)}, u32[]{:S(2)}, u32[]{:S(2)}) %all-to-all-start.3) | async-done | bytes 983072 | tf_op jit(solution)/shard_map/all_to_all | solution.py:110
  384.1 5.2 %all-to-all-start.1 = ((bf16[128,30,128]{2,1,0:T(8,128)(2,1)}), bf16[128,30,128]{2,1,0:T(8,128)(2,1)}, u32[]{:S(2)}, u32[]{:S(2)}) async-start(bf16[128,30,128]{2,1,0:T(8,128)(2,1)} %bitcast.52), calls=%async_computation.1 | async-start | bytes 2097152 | tf_op jit(solution)/shard_map/all_to_all | solution.py:110
  389.4 2.6 copy.230
  394.0 4.2 multiply_convert_fusion.2
  398.3 2.7 copy.235
  420.4 3.6 pad_slice_fusion
  425.7 10.6 %all-to-all-start.4 = ((f32[128,1,2688]{2,1,0:T(1,128)}), f32[128,1,2688]{2,1,0:T(1,128)}, u32[]{:S(2)}, u32[]{:S(2)}) async-start(f32[128,1,2688]{2,1,0:T(1,128)} %bitcast.397), calls=%async_computation.4 | async-start | bytes 2752512 | tf_op jit(solution)/shard_map/all_to_all | solution.py:117
  436.4 3.6 convolution_add_fusion.7
  450.8 7.6 %all-to-all-done.4 = f32[128,1,2688]{2,1,0:T(1,128)} async-done(((f32[128,1,2688]{2,1,0:T(1,128)}), f32[128,1,2688]{2,1,0:T(1,128)}, u32[]{:S(2)}, u32[]{:S(2)}) %all-to-all-start.4) | async-done | bytes 1376288 | tf_op jit(solution)/shard_map/all_to_all | solution.py:117
  462.4 4.3 all-to-all-start.5
  473.4 15.9 %all-to-all-done.5 = f32[128,1,2688]{2,1,0:T(1,128)S(1)} async-done(((f32[128,1,2688]{2,1,0:T(1,128)}), f32[128,1,2688]{2,1,0:T(1,128)S(1)}, u32[]{:S(2)}, u32[]{:S(2)}) %all-to-all-start.5) | async-done | bytes 1376288 | tf_op jit(solution)/shard_map/all_to_all | solution.py:122
  (229 shorter events, 174.2 us)
Async XLA Ops:
  0.6 7.3 %copy-start.40 = (bf16[9,128,128]{2,1,0:T(8,128)(2,1)S(1)}, bf16[9,128,128]{2,1,0:T(8,128)(2,1)}, u32[]{:S(2)}) copy-start(bf16[9,128,128]{2,1,0:T(8,128)(2,1)} %param.8) | copy-start | bytes 884740
  12.4 62.6 %copy-start = (f32[3840,128]{1,0:T(8,128)}, f32[3840,128]{1,0:T(8,128)S(1)}, u32[]{:S(2)}) copy-start(f32[3840,128]{1,0:T(8,128)S(1)} %convolution_add_fusion.24) | copy-start | bytes 5898244
  52.6 15.3 %copy-start.51 = (s32[2]{0:T(128)S(1)}, s32[2]{0:T(128)}, u32[]{:S(2)}) copy-start(s32[2]{0:T(128)} %param.12) | copy-start | bytes 28
  55.6 58.8 %all-to-all-start = ((bf16[128,2,1920]{2,1,0:T(2,128)(2,1)}), bf16[128,2,1920]{2,1,0:T(2,128)(2,1)}, u32[]{:S(2)}, u32[]{:S(2)}) async-start(bf16[128,2,1920]{2,1,0:T(2,128)(2,1)} %reshape.597), calls=%async_computation | async-start | bytes 1966080 | tf_op jit(solution)/shard_map/all_to_all | solution.py:106
  86.4 26.1 %copy-start.18 = (f32[128,30,128]{2,1,0:T(8,128)S(1)}, f32[128,30,128]{2,1,0:T(8,128)}, u32[]{:S(2)}) copy-start(f32[128,30,128]{2,1,0:T(8,128)} %reshape.556) | copy-start | bytes 5898244
  112.5 1.9 copy-start.52
  114.4 108.4 %all-to-all-start.2 = ((bf16[128,2,1920]{2,1,0:T(2,128)(2,1)}), bf16[128,2,1920]{2,1,0:T(2,128)(2,1)}, u32[]{:S(2)}, u32[]{:S(2)}) async-start(bf16[128,2,1920]{2,1,0:T(2,128)(2,1)} %reshape.599), calls=%async_computation.2 | async-start | bytes 1966080 | tf_op jit(solution)/shard_map/all_to_all | solution.py:106
  129.4 50.3 %copy-start.4 = (bf16[3840,1,128]{2,1,0:T(2,128)(2,1)}, bf16[3840,1,128]{2,1,0:T(2,128)(2,1)S(1)}, u32[]{:S(2)}) copy-start(bf16[3840,1,128]{2,1,0:T(2,128)(2,1)S(1)} %reshape.598) | copy-start | bytes 2949124
  176.8 1.7 copy-start.31
  191.2 4.1 copy-start.3
  195.3 4.9 copy-start.14
  200.2 4.2 copy-start.12
  204.3 3.4 copy-start.16
  247.1 3.6 copy-start.49
  263.3 3.0 copy-start.17
  288.9 1.7 copy-start.29
  290.6 1.6 copy-start.20
  290.7 2.1 copy-start.38
  294.4 1.6 copy-start.37
  294.4 1.8 copy-start.44
  305.0 3.0 copy-start.10
  314.8 3.0 copy-start.47
  321.6 3.1 copy-start.15
  321.6 4.1 copy-start.41
  321.6 4.1 copy-start.53
  324.7 2.5 copy-start.13
  325.7 2.5 copy-start.11
  327.1 2.1 copy-start.9
  328.2 2.1 copy-start.5
  328.2 2.1 copy-start.42
  329.3 2.1 copy-start.8
  345.3 1.7 copy-start.30
  353.0 13.5 %copy-start.7 = (bf16[128,30,128]{0,2,1:T(8,128)(2,1)S(1)}, bf16[128,30,128]{0,2,1:T(8,128)(2,1)}, u32[]{:S(2)}) copy-start(bf16[128,30,128]{0,2,1:T(8,128)(2,1)} %get-tuple-element.27) | copy-start | bytes 2949124
  355.3 28.8 %all-to-all-start.3 = ((bf16[128,30,128]{2,1,0:T(8,128)(2,1)}), bf16[128,30,128]{2,1,0:T(8,128)(2,1)}, u32[]{:S(2)}, u32[]{:S(2)}) async-start(bf16[128,30,128]{2,1,0:T(8,128)(2,1)} %convert_element_type.195), calls=%async_computation.3 | async-start | bytes 2097152 | tf_op jit(solution)/shard_map/all_to_all | solution.py:110
  365.5 2.1 copy-start.48
  365.5 3.9 copy-start.50
  365.5 4.1 copy-start.21
  384.1 41.6 %all-to-all-start.1 = ((bf16[128,30,128]{2,1,0:T(8,128)(2,1)}), bf16[128,30,128]{2,1,0:T(8,128)(2,1)}, u32[]{:S(2)}, u32[]{:S(2)}) async-start(bf16[128,30,128]{2,1,0:T(8,128)(2,1)} %bitcast.52), calls=%async_computation.1 | async-start | bytes 2097152 | tf_op jit(solution)/shard_map/all_to_all | solution.py:110
  394.0 20.2 %copy-start.2 = (f32[128,30,128]{2,1,0:T(8,128)}, f32[128,30,128]{2,1,0:T(8,128)S(1)}, u32[]{:S(2)}) copy-start(f32[128,30,128]{2,1,0:T(8,128)S(1)} %copy.231) | copy-start | bytes 5898244
  403.1 2.4 copy-start.33
  414.2 1.5 copy-start.36
  415.7 2.4 copy-start.1
  425.7 32.7 %all-to-all-start.4 = ((f32[128,1,2688]{2,1,0:T(1,128)}), f32[128,1,2688]{2,1,0:T(1,128)}, u32[]{:S(2)}, u32[]{:S(2)}) async-start(f32[128,1,2688]{2,1,0:T(1,128)} %bitcast.397), calls=%async_computation.4 | async-start | bytes 2752512 | tf_op jit(solution)/shard_map/all_to_all | solution.py:117
  444.7 2.4 copy-start.26
  447.1 1.5 copy-start.39
  460.6 6.1 %copy-start.23 = (bf16[1,32,120,128]{3,2,1,0:T(8,128)(2,1)S(1)}, bf16[1,32,120,128]{3,2,1,0:T(8,128)(2,1)}, u32[]{:S(2)}) copy-start(bf16[1,32,120,128]{3,2,1,0:T(8,128)(2,1)} %get-tuple-element.11) | copy-start | bytes 2949124
  462.4 26.8 %all-to-all-start.5 = ((f32[128,1,2688]{2,1,0:T(1,128)}), f32[128,1,2688]{2,1,0:T(1,128)S(1)}, u32[]{:S(2)}, u32[]{:S(2)}) async-start(f32[128,1,2688]{2,1,0:T(1,128)} %broadcast_in_dim.5), calls=%async_computation.5 | async-start | bytes 2752512 | tf_op jit(solution)/shard_map/all_to_all | solution.py:122
  466.7 2.1 copy-start.22
  (12 other events, 15.2 us)
where the time goes:
time: 502 us; the launch traced here: 492 us
  local copies, waits for them, and re-layouts  235 us (47%)
  matrix products  87.9 us (18%)
  other arithmetic  70.9 us (14%)
  starting transfers between devices  53.4 us (11%)
  waiting for transfers between devices  36.5 us (7%)
  between operations  8.25 us (2%)
    dynamic_slice x20, local copies, waits for them, and re-layouts, shifted(): return lax.dynamic_slice_in_dim(padded, start, values.shape[0], 0)  53.4 us
    unnamed x2, other arithmetic  46.2 us
    all_to_all x4, local copies, waits for them, and re-layouts, to_pixels(): lax.all_to_all(flat, ('seg', 'grp'), split_axis=1, concat_axis=0, tiled=T...  40.8 us
    dot_general x21, matrix products, inner(): lax.dot_general(left, right, (((0,), (0,)), ((), ())), preferred_element_...  28.1 us
    all_to_all x2, starting transfers between devices, to_pixels(): lax.all_to_all(flat, ('seg', 'grp'), split_axis=1, concat_axis=0, tiled=T...  23 us
    unnamed x113, local copies, waits for them, and re-layouts  21.1 us
    dot_general x9, matrix products, spatial_back(): jnp.dot(piece, kernel[3 * row_tap + col_tap].T, preferred_element_type=jn...  17 us
    dot_general x10, matrix products, temporal_back(): jnp.dot(piece, kernel[tap].T, preferred_element_type=jnp.float32)  16.8 us
  transfers between devices with their start and end apart: 6, of which 3 were waited for; matrix products, arithmetic and copies ran while one was open for 40% of the time, Pallas kernels for 0%

commit v1 on v0

--- a/solution.py
+++ b/solution.py
@@ -107,7 +107,15 @@
 
 
 def to_frames(blocks):
-    return lax.all_to_all(blocks, ("seg", "grp"), split_axis=0, concat_axis=1, tiled=True)
+    return jnp.concatenate(
+        lax.all_to_all(
+            jnp.stack(jnp.split(blocks, lax.axis_size(("seg", "grp")), axis=0)),
+            ("seg", "grp"),
+            0,
+            0,
+        ),
+        1,
+    )
 
 
 def all_sum(parts):

time: 502 us -> 615 us (1.23)
  local copies, waits for them, and re-layouts: 235 us -> 371 us
  matrix products: 87.9 us -> 71.7 us
    unnamed x113 -> x379, local copies, waits for them, and re-layouts: 21.1 us -> 176 us
    dot_general x21, matrix products: 28.1 us -> 16.1 us  [inner(): lax.dot_general(left, right, (((0,), (0,)), ((), ())), preferred_element_...]
  transfers between devices with their start and end apart: 6 -> 6, of which waited for: 3 -> 3; matrix products, arithmetic and copies ran while one was open for 40% -> 29% of each run, Pallas kernels for 0% -> 0%
where the time goes in v1:
time: 615 us; the launch traced here: 606 us
  local copies, waits for them, and re-layouts  371 us (60%)
  matrix products  71.7 us (12%)
  other arithmetic  66.1 us (11%)
  starting transfers between devices  52.4 us (9%)
  waiting for transfers between devices  35.9 us (6%)
  between operations  8.81 us (1%)
    unnamed x379, local copies, waits for them, and re-layouts  176 us
    dynamic_slice x20, local copies, waits for them, and re-layouts, shifted(): return lax.dynamic_slice_in_dim(padded, start, values.shape[0], 0)  49.4 us
    unnamed x2, other arithmetic  44.3 us
    all_to_all x4, local copies, waits for them, and re-layouts, to_pixels(): lax.all_to_all(flat, ('seg', 'grp'), split_axis=1, concat_axis=0, tiled=T...  37.9 us
    all_to_all x2, starting transfers between devices, to_pixels(): lax.all_to_all(flat, ('seg', 'grp'), split_axis=1, concat_axis=0, tiled=T...  22.7 us
    all_to_all x1, waiting for transfers between devices, all_sum(): lax.all_to_all(spread, ('seg', 'grp'), split_axis=0, concat_axis=0, tiled...  16.7 us
    reshape x8, local copies, waits for them, and re-layouts, temporal_forward(): piece = shifted(acts, (tap - 2) * step_size).reshape(-1, chans)  16.7 us
    dot_general x21, matrix products, inner(): lax.dot_general(left, right, (((0,), (0,)), ((), ())), preferred_element_...  16.1 us
  transfers between devices with their start and end apart: 6, of which 3 were waited for; matrix products, arithmetic and copies ran while one was open for 29% of the time, Pallas kernels for 0%

profile of v1, /device:TPU:1, one launch (start us, length us, event | category | flops | bytes accessed | tf_op | source)
XLA Modules:
  0.0 605.6 jit_solution(16425901323556292564)
XLA Ops:
  0.6 7.3 %pad_slice_fusion.8 = (bf16[1,32,120,128]{3,2,1,0:T(8,128)(2,1)S(1)}, bf16[1,32,120,128]{3,2,1,0:T(8,128)(2,1)S(1)}, bf16[1,32,120,128]{3,2,1,0:T(8,128)(2,1)S(1...) fusion(bf16[1,32,120,128]{3,2,1,0:T(8,128)(2,1)} %param.7), kind=kLoop, calls=%fused_computation.150 | loop fusion | bytes 8847360 | tf_op jit(solution)/shard_map/slice | solution.py:32
  12.9 16.0 %copy.618 = bf16[1,3840,128]{2,0,1:T(2,128)(2,1)} copy(bf16[1,3840,128]{2,1,0:T(8,128)(2,1)S(1)} %fusion.47) | data formatting | bytes 1966080 | tf_op jit(solution)/shard_map/convert_element_type | solution.py:147
  29.5 22.3 %reduce.5 = bf16[3840,128]{1,0:T(8,128)(2,1)S(1)} reduce(bf16[3840,1,128]{2,1,0:T(2,128)(2,1)} %bitcast.1440, bf16[]{:T(256)} %broadcast.166), dimensions={1}, to_apply=%bitcast.1432.reduce_sub_computation | reduce | bytes 1966082
  53.1 11.9 %all-to-all-start = ((bf16[128,2,1920]{2,1,0:T(2,128)(2,1)}), bf16[128,2,1920]{2,1,0:T(2,128)(2,1)S(1)}, u32[]{:S(2)}, u32[]{:S(2)}) async-start(bf16[128,2,1920]{2,1,0:T(2,128)(2,1)} %reshape.863), calls=%async_computation | async-start | bytes 1966080 | tf_op jit(solution)/shard_map/all_to_all | solution.py:106
  73.5 9.1 %copy.617 = bf16[1,3840,128]{2,0,1:T(2,128)(2,1)S(1)} copy(bf16[1,3840,128]{2,1,0:T(8,128)(2,1)} %bitcast.1592) | data formatting | bytes 1966080 | tf_op jit(solution)/shard_map/reshape | solution.py:148
  82.6 22.0 %reduce.6 = bf16[3840,128]{1,0:T(8,128)(2,1)} reduce(bf16[3840,1,128]{2,1,0:T(2,128)(2,1)S(1)} %bitcast.1441, bf16[]{:T(256)} %broadcast.166), dimensions={1}, to_apply=%bitcast.1431.reduce_sub_computation | reduce | bytes 1966082
  104.6 3.0 reshape.865
  108.7 10.8 %all-to-all-start.2 = ((bf16[128,2,1920]{2,1,0:T(2,128)(2,1)}), bf16[128,2,1920]{2,1,0:T(2,128)(2,1)}, u32[]{:S(2)}, u32[]{:S(2)}) async-start(bf16[128,2,1920]{2,1,0:T(2,128)(2,1)} %reshape.865), calls=%async_computation.2 | async-start | bytes 1966080 | tf_op jit(solution)/shard_map/all_to_all | solution.py:106
  119.5 4.1 reshape.864
  123.7 16.4 %bitcast_reduce_fusion.1 = bf16[3840,128]{1,0:T(8,128)(2,1)S(1)} fusion(bf16[3840,1,128]{2,1,0:T(2,128)(2,1)S(1)} %reshape.864), kind=kLoop, calls=%fused_computation.780 | loop fusion | bytes 1966080 | tf_op jit(solution)/shard_map/all_to_all | solution.py:106
  141.3 2.6 copy.530
  144.0 5.5 pad_dynamic-slice_fusion.12
  153.7 2.7 copy.532
  158.6 2.7 copy.533
  163.4 2.7 copy.531
  173.8 2.6 multiply_convert_fusion.9
  177.7 2.7 reshape.792
  183.2 3.5 pad_dynamic-slice_fusion.8
  186.8 2.8 copy.540
  208.5 3.0 multiply_convert_fusion.8
  211.5 2.7 reshape.797
  214.1 2.7 reshape.801
  216.8 5.6 reshape.866
  222.5 17.6 %bitcast_reduce_fusion = bf16[3840,128]{1,0:T(8,128)(2,1)S(1)} fusion(bf16[3840,1,128]{2,1,0:T(2,128)(2,1)} %reshape.866), kind=kLoop, calls=%fused_computation.779 | loop fusion | bytes 1966080 | tf_op jit(solution)/shard_map/all_to_all | solution.py:106
  243.0 5.0 multiply_convert_fusion
  248.0 2.6 reshape.804
  250.6 3.0 copy.544
  253.6 2.9 copy.542
  256.5 2.9 multiply_convert_fusion.7
  260.4 3.5 pad_dynamic-slice_fusion.4
  270.3 2.3 copy.547
  284.4 3.2 multiply_convert_fusion.4
  287.6 2.7 reshape.807
  290.3 2.9 copy.550
  293.2 3.0 multiply_convert_fusion.5
  297.2 3.4 pad_dynamic-slice_fusion
  302.8 3.0 convolution_bitcast_fusion.1
  309.9 3.0 convolution_bitcast_fusion
  485.7 9.8 %all-to-all-start.3 = ((bf16[128,1,30,128]{3,2,1,0:T(8,128)(2,1)}), bf16[128,1,30,128]{3,2,1,0:T(8,128)(2,1)S(1)}, u32[]{:S(2)}, u32[]{:S(2)}) async-start(bf16[128,1,30,128]{3,2,1,0:T(8,128)(2,1)} %constant_dynamic-update-slice_fusion.128), calls=%async_computation.3 | async-start | bytes 2097152 | tf_op jit(solution)/shard_map/all_to_all | solution.py:111
  504.3 10.2 %all-to-all-done.3 = bf16[128,1,30,128]{3,2,1,0:T(8,128)(2,1)S(1)} async-done(((bf16[128,1,30,128]{3,2,1,0:T(8,128)(2,1)}), bf16[128,1,30,128]{3,2,1,0:T(8,128)(2,1)S(1)}, u32[]{:S(2)}, u32[]{:S(2)}) %all-to-all-start.3) | async-done | bytes 983072 | tf_op jit(solution)/shard_map/all_to_all | solution.py:111
  514.4 5.0 all-to-all-start.1
  528.3 3.3 reshape.837
  533.9 3.5 pad_slice_fusion
  539.1 10.7 %all-to-all-start.4 = ((f32[128,1,2688]{2,1,0:T(1,128)}), f32[128,1,2688]{2,1,0:T(1,128)}, u32[]{:S(2)}, u32[]{:S(2)}) async-start(f32[128,1,2688]{2,1,0:T(1,128)} %bitcast.1443), calls=%async_computation.4 | async-start | bytes 2752512 | tf_op jit(solution)/shard_map/all_to_all | solution.py:125
  549.9 3.6 convolution_add_fusion.7
  563.0 9.0 %all-to-all-done.4 = f32[128,1,2688]{2,1,0:T(1,128)} async-done(((f32[128,1,2688]{2,1,0:T(1,128)}), f32[128,1,2688]{2,1,0:T(1,128)}, u32[]{:S(2)}, u32[]{:S(2)}) %all-to-all-start.4) | async-done | bytes 1376288 | tf_op jit(solution)/shard_map/all_to_all | solution.py:125
  575.9 4.3 all-to-all-start.5
  586.0 16.7 %all-to-all-done.5 = f32[128,1,2688]{2,1,0:T(1,128)S(1)} async-done(((f32[128,1,2688]{2,1,0:T(1,128)}), f32[128,1,2688]{2,1,0:T(1,128)S(1)}, u32[]{:S(2)}, u32[]{:S(2)}) %all-to-all-start.5) | async-done | bytes 1376288 | tf_op jit(solution)/shard_map/all_to_all | solution.py:130
  (492 shorter events, 295.0 us)
Async XLA Ops:
  0.6 7.3 %copy-start.42 = (bf16[9,128,128]{2,1,0:T(8,128)(2,1)S(1)}, bf16[9,128,128]{2,1,0:T(8,128)(2,1)}, u32[]{:S(2)}) copy-start(bf16[9,128,128]{2,1,0:T(8,128)(2,1)} %param.8) | copy-start | bytes 884740
  12.4 59.6 %copy-start = (f32[3840,128]{1,0:T(8,128)}, f32[3840,128]{1,0:T(8,128)S(1)}, u32[]{:S(2)}) copy-start(f32[3840,128]{1,0:T(8,128)S(1)} %convolution_add_fusion.24) | copy-start | bytes 5898244
  51.8 13.1 %copy-start.57 = (s32[2]{0:T(128)S(1)}, s32[2]{0:T(128)}, u32[]{:S(2)}) copy-start(s32[2]{0:T(128)} %param.12) | copy-start | bytes 28
  53.1 54.7 %all-to-all-start = ((bf16[128,2,1920]{2,1,0:T(2,128)(2,1)}), bf16[128,2,1920]{2,1,0:T(2,128)(2,1)S(1)}, u32[]{:S(2)}, u32[]{:S(2)}) async-start(bf16[128,2,1920]{2,1,0:T(2,128)(2,1)} %reshape.863), calls=%async_computation | async-start | bytes 1966080 | tf_op jit(solution)/shard_map/all_to_all | solution.py:106
  82.6 25.1 %copy-start.58 = (s32[8]{0:T(128)S(1)}, s32[8]{0:T(128)}, u32[]{:S(2)}) copy-start(s32[8]{0:T(128)} %param.11) | copy-start | bytes 100
  108.7 108.1 %all-to-all-start.2 = ((bf16[128,2,1920]{2,1,0:T(2,128)(2,1)}), bf16[128,2,1920]{2,1,0:T(2,128)(2,1)}, u32[]{:S(2)}, u32[]{:S(2)}) async-start(bf16[128,2,1920]{2,1,0:T(2,128)(2,1)} %reshape.865), calls=%async_computation.2 | async-start | bytes 1966080 | tf_op jit(solution)/shard_map/all_to_all | solution.py:106
  123.7 47.5 %copy-start.3 = (bf16[3840,1,128]{2,1,0:T(2,128)(2,1)}, bf16[3840,1,128]{2,1,0:T(2,128)(2,1)S(1)}, u32[]{:S(2)}) copy-start(bf16[3840,1,128]{2,1,0:T(2,128)(2,1)S(1)} %reshape.864) | copy-start | bytes 2949124
  168.3 1.7 copy-start.31
  176.4 1.3 copy-start.23
  182.7 4.1 copy-start.2
  186.8 4.9 copy-start.12
  191.7 4.2 copy-start.10
  195.9 4.2 copy-start.15
  240.1 2.6 copy-start.55
  277.0 1.7 copy-start.30
  278.7 1.6 copy-start.17
  278.7 2.1 copy-start.40
  280.9 1.7 copy-start.27
  282.6 1.6 copy-start.39
  282.6 1.8 copy-start.46
  293.2 3.0 copy-start.14
  302.8 3.0 copy-start.49
  309.9 3.0 copy-start.19
  313.0 74.3 %copy-start.13 = (bf16[128,30,128]{0,2,1:T(8,128)(2,1)S(1)}, bf16[128,30,128]{0,2,1:T(8,128)(2,1)}, u32[]{:S(2)}) copy-start(bf16[128,30,128]{0,2,1:T(8,128)(2,1)} %get-tuple-element.24) | copy-start | bytes 2949124
  313.0 74.3 %copy-start.51 = (f32[5,128,128]{2,1,0:T(8,128)S(1)}, f32[5,128,128]{2,1,0:T(8,128)}, u32[]{:S(2)}) copy-start(f32[5,128,128]{2,1,0:T(8,128)} %fusion.13) | copy-start | bytes 983044
  313.4 74.3 %copy-start.18 = (bf16[8,16,30,128]{3,2,1,0:T(8,128)(2,1)}, bf16[8,16,30,128]{3,2,1,0:T(8,128)(2,1)S(1)}, u32[]{:S(2)}) copy-start(bf16[8,16,30,128]{3,2,1,0:T(8,128)(2,1)S(1)} %add_convert_fusion) | copy-start | bytes 2949124
  318.2 69.5 %copy-start.43 = (bf16[128,30,128]{2,1,0:T(8,128)(2,1)S(1)}, bf16[128,30,128]{2,1,0:T(8,128)(2,1)}, u32[]{:S(2)}) copy-start(bf16[128,30,128]{2,1,0:T(8,128)(2,1)} %convert_element_type.204) | copy-start | bytes 2949124
  318.2 69.5 %copy-start.59 = (bf16[8,16,30,128]{3,2,1,0:T(8,128)(2,1)S(1)}, bf16[8,16,30,128]{3,2,1,0:T(8,128)(2,1)}, u32[]{:S(2)}) copy-start(bf16[8,16,30,128]{3,2,1,0:T(8,128)(2,1)} %get-tuple-element.5) | copy-start | bytes 2949124
  388.6 1.3 copy-start.53
  389.0 1.6 copy-start.4
  389.0 1.9 copy-start.44
  389.9 1.5 copy-start.52
  389.9 1.5 copy-start.7
  393.0 3.2 copy-start.34
  396.2 1.6 copy-start.33
  466.5 31.0 %copy-start.56 = (f32[1,128,128]{2,1,0:T(8,128)S(1)}, f32[1,128,128]{2,1,0:T(8,128)}, u32[]{:S(2)}) copy-start(f32[1,128,128]{2,1,0:T(8,128)} %convolution_bitcast_fusion.1) | copy-start | bytes 196612
  485.7 28.7 %all-to-all-start.3 = ((bf16[128,1,30,128]{3,2,1,0:T(8,128)(2,1)}), bf16[128,1,30,128]{3,2,1,0:T(8,128)(2,1)S(1)}, u32[]{:S(2)}, u32[]{:S(2)}) async-start(bf16[128,1,30,128]{3,2,1,0:T(8,128)(2,1)} %constant_dynamic-update-slice_fusion.128), calls=%async_computation.3 | async-start | bytes 2097152 | tf_op jit(solution)/shard_map/all_to_all | solution.py:111
  495.5 23.9 %copy-start.16 = (f32[128,1,30,128]{3,2,0,1:T(8,128)S(1)}, f32[128,1,30,128]{3,2,0,1:T(8,128)}, u32[]{:S(2)}) copy-start(f32[128,1,30,128]{3,2,0,1:T(8,128)} %reshape.822) | copy-start | bytes 5898244
  514.4 24.7 %all-to-all-start.1 = ((bf16[128,1,30,128]{3,2,1,0:T(8,128)(2,1)}), bf16[128,1,30,128]{3,2,1,0:T(8,128)(2,1)}, u32[]{:S(2)}, u32[]{:S(2)}) async-start(bf16[128,1,30,128]{3,2,1,0:T(8,128)(2,1)} %constant_dynamic-update-slice_fusion), calls=%async_computation.1 | async-start | bytes 2097152 | tf_op jit(solution)/shard_map/all_to_all | solution.py:111
  521.2 1.5 copy-start.6
  528.3 3.3 copy-start.1
  539.1 32.8 %all-to-all-start.4 = ((f32[128,1,2688]{2,1,0:T(1,128)}), f32[128,1,2688]{2,1,0:T(1,128)}, u32[]{:S(2)}, u32[]{:S(2)}) async-start(f32[128,1,2688]{2,1,0:T(1,128)} %bitcast.1443), calls=%async_computation.4 | async-start | bytes 2752512 | tf_op jit(solution)/shard_map/all_to_all | solution.py:125
  555.0 2.2 copy-start.26
  557.2 2.1 copy-start.25
  559.3 1.5 copy-start.41
  574.1 6.1 %copy-start.22 = (bf16[1,32,120,128]{3,2,1,0:T(8,128)(2,1)S(1)}, bf16[1,32,120,128]{3,2,1,0:T(8,128)(2,1)}, u32[]{:S(2)}) copy-start(bf16[1,32,120,128]{3,2,1,0:T(8,128)(2,1)} %get-tuple-element.11) | copy-start | bytes 2949124
  575.9 26.8 %all-to-all-start.5 = ((f32[128,1,2688]{2,1,0:T(1,128)}), f32[128,1,2688]{2,1,0:T(1,128)S(1)}, u32[]{:S(2)}, u32[]{:S(2)}) async-start(f32[128,1,2688]{2,1,0:T(1,128)} %broadcast_in_dim.5), calls=%async_computation.5 | async-start | bytes 2752512 | tf_op jit(solution)/shard_map/all_to_all | solution.py:130
  580.2 2.1 copy-start.21
  (18 other events, 21.5 us)
